TPU v7x, 32 devices: a whole 2x2x4 slice. The times are simulated.
32 devices in a mesh: az: 16 (over z, x, core), el: 2 (over y).
Axes of the slice: x: 2, y: 2, z: 4, core: 2. Of those that a mesh axis runs over, the one named last changes fastest.
Arguments:
- raw_sweeps: bfloat16 [4, 1, 24, 96, 256], P('el', None, None, 'az'), may hold values from -6 to 6
- sweep_ids: int32 [4], P('el'), may hold values from 0 to 3, each once
- elevation_embed: float32 [4, 128], replicated, may hold values from -3 to 3
- input_proj: bfloat16 [24, 128], replicated, may hold values from -0.875 to 0.875
- first_kernel: bfloat16 [3, 3, 128, 128], replicated, may hold values from -0.1875 to 0.1875
- second_kernel: bfloat16 [3, 3, 128, 128], replicated, may hold values from -0.1875 to 0.1875
- join_weight: bfloat16 [2, 128, 128], P('el'), may hold values from -0.375 to 0.375
- head_weight: bfloat16 [12, 128], replicated, may hold values from -0.5 to 0.5
- cotangent: bfloat16 [1, 12, 96, 256], P(None, None, 'az'), may hold values from -6 to 6
Outputs:
- prediction: float32 [1, 12, 96, 256], P(None, None, 'az')
- join_grad: float32 [2, 128, 128], P('el')
- first_kernel_gradient: float32 [3, 3, 128, 128], replicated
- second_kernel_gradient: float32 [3, 3, 128, 128], replicated
- input_grad: float32 [24, 128], replicated
- embed_grad: float32 [4, 128], replicated
Inputs may be any that keep to these rules, and one draw needn't show every extreme that they name: `sweep_ids`: each sweep fills exactly one slot.
All inputs are finite; a program needn't handle non-finite values.
Results may differ from a plain program's by a relative error of at most 0.023.
Values may be sent and summed in bfloat16 or wider, within the bound.
A program may use at most 64 MiB of HBM per device.

v0:
```python
import math
import jax
import jax.numpy as jnp
from jax import lax
from jax.sharding import PartitionSpec as P

CHANNELS = 128
FIRST_DILATION = 1
SECOND_DILATION = 2
precise = lax.Precision.HIGHEST


def padded_2(block, sides, width):
    for axis, dim in sides:
        count = lax.axis_size(axis)
        forward = [(i, i + 1) for i in range(count - 1)]
        forward.append((count - 1, 0))
        backward = [(target, source) for source, target in forward]
        low = lax.ppermute(
            lax.slice_in_dim(block, block.shape[dim] - width, None, axis=dim), axis, forward
        )
        high = lax.ppermute(lax.slice_in_dim(block, 0, width, axis=dim), axis, backward)
        block = jnp.concatenate([low, block, high], axis=dim)
    return block


def silu_slope(values):
    logistic = jax.nn.sigmoid(values)
    return logistic * (1.0 + values * (1.0 - logistic))


def range_padding(source, dilate):
    return jnp.pad(source, ((0, 0), (0, 0), (0, 0), (dilate, dilate)))


def convolve_partial(padded, kernel, dilate):
    return lax.conv_general_dilated(
        padded,
        kernel,
        (1, 1),
        "VALID",
        rhs_dilation=(dilate, dilate),
        dimension_numbers=("NCHW", "HWIO", "NCHW"),
        preferred_element_type=jnp.float32,
    )


def reversed_kernel(kernel):
    return jnp.flip(kernel, (0, 1)).transpose(0, 1, 3, 2)


def kernel_gradient_of(padded, upstream, dilate):
    ray_count = upstream.shape[2]
    gate_count = upstream.shape[3]
    tap_rows = []
    for tap_row in range(3):
        tap_line = []
        for tap_column in range(3):
            window = padded[
                :,
                :,
                tap_row * dilate : tap_row * dilate + ray_count,
                tap_column * dilate : tap_column * dilate + gate_count,
            ]
            tap_line.append(
                jnp.einsum("niar,noar->io", window, upstream, preferred_element_type=jnp.float32)
            )
        tap_rows.append(jnp.stack(tap_line))
    return jnp.stack(tap_rows)


def activate(source):
    return jax.nn.silu(source.astype(jnp.float32)).astype(jnp.bfloat16)


def shards(
    raw_sweeps,
    sweep_ids,
    elevation_embed,
    input_proj,
    first_kernel,
    second_kernel,
    join_weight,
    head_weight,
    cotangent,
):
    brain_float_half = jnp.bfloat16
    sweep_total = elevation_embed.shape[0]
    onehot = (sweep_ids[:, None] == jnp.arange(sweep_total, dtype=jnp.int32)[None, :]).astype(
        jnp.float32
    )
    bias_rows = jnp.dot(onehot, elevation_embed, precision=precise)
    group_bias = jnp.sum(bias_rows, axis=0)
    input_state = jnp.einsum(
        "jbiar,ic->bcar", raw_sweeps, input_proj, preferred_element_type=jnp.float32
    )
    input_state = (input_state + group_bias[None, :, None, None]).astype(brain_float_half)
    input_activation = activate(input_state)
    padded_input = range_padding(
        padded_2(input_activation, (("az", 2),), FIRST_DILATION), FIRST_DILATION
    )
    hidden_state = (
        input_state.astype(jnp.float32)
        + convolve_partial(padded_input, first_kernel, FIRST_DILATION)
    ).astype(brain_float_half)
    hidden_activation = activate(hidden_state)
    padded_hidden = range_padding(
        padded_2(hidden_activation, (("az", 2),), SECOND_DILATION), SECOND_DILATION
    )
    final_state = (
        hidden_state.astype(jnp.float32)
        + convolve_partial(padded_hidden, second_kernel, SECOND_DILATION)
    ).astype(brain_float_half)
    group_weight = join_weight[0]
    empty_sum = jnp.zeros((CHANNELS,) + final_state.shape[:1] + final_state.shape[2:], jnp.float32)
    joined_all = (
        empty_sum
        + jnp.einsum(
            "gbiar,gio->obar",
            lax.all_gather(final_state[None], "el", axis=0, tiled=True),
            lax.all_gather(join_weight, "el", axis=0, tiled=True),
            preferred_element_type=jnp.float32,
        )
    ).astype(brain_float_half)
    prediction = jnp.einsum(
        "lc,cbar->blar", head_weight, joined_all, preferred_element_type=jnp.float32
    )
    ray_total = final_state.shape[2] * lax.axis_size("az")
    grad_scale = 1.0 / math.sqrt(
        lax.axis_size("el") * final_state.shape[0] * ray_total * final_state.shape[3]
    )
    joined_back = jnp.einsum(
        "lc,blar->bcar", head_weight, cotangent, preferred_element_type=jnp.float32
    ).astype(brain_float_half)
    join_local = jnp.einsum(
        "biar,boar->io", final_state, joined_back, preferred_element_type=jnp.float32
    )
    join_total = lax.psum(join_local, "az")
    grad_two = jnp.einsum(
        "io,boar->biar", group_weight, joined_back, preferred_element_type=jnp.float32
    )
    final_upstream_gradient = grad_two.astype(brain_float_half)
    second_kernel_partial = kernel_gradient_of(
        padded_hidden, final_upstream_gradient, SECOND_DILATION
    )
    second_border_rays = range_padding(
        padded_2(final_upstream_gradient, (("az", 2),), SECOND_DILATION), SECOND_DILATION
    )
    second_backward_pass = convolve_partial(
        second_border_rays, reversed_kernel(second_kernel), SECOND_DILATION
    )
    grad_one = grad_two + second_backward_pass * silu_slope(hidden_state.astype(jnp.float32))
    hidden_upstream_gradient = grad_one.astype(brain_float_half)
    first_kernel_partial = kernel_gradient_of(
        padded_input, hidden_upstream_gradient, FIRST_DILATION
    )
    first_border_rays = range_padding(
        padded_2(hidden_upstream_gradient, (("az", 2),), FIRST_DILATION), FIRST_DILATION
    )
    first_backward_pass = convolve_partial(
        first_border_rays, reversed_kernel(first_kernel), FIRST_DILATION
    )
    grad_zero = (
        grad_one + first_backward_pass * silu_slope(input_state.astype(jnp.float32))
    ).astype(brain_float_half)
    input_local = jnp.einsum(
        "jbiar,bcar->ic", raw_sweeps, grad_zero, preferred_element_type=jnp.float32
    )
    column_sum = jnp.sum(grad_zero.astype(jnp.float32), axis=(0, 2, 3))
    slot_terms = jnp.broadcast_to(column_sum[None, :], (raw_sweeps.shape[0], column_sum.shape[0]))
    embed_local = jnp.dot(onehot.T, slot_terms, precision=precise)
    second_total, first_total, input_total, embed_total = lax.psum(
        (second_kernel_partial, first_kernel_partial, input_local, embed_local), ("az", "el")
    )
    return (
        prediction,
        join_total[None] * grad_scale,
        first_total * grad_scale,
        second_total * grad_scale,
        input_total * grad_scale,
        embed_total * grad_scale,
    )


def solution(mesh):
    in_specs = (
        P("el", None, None, "az", None),
        P("el"),
        P(),
        P(),
        P(),
        P(),
        P("el", None, None),
        P(),
        P(None, None, "az", None),
    )
    out_specs = (P(None, None, "az", None), P("el", None, None), P(), P(), P(), P())
    return jax.shard_map(shards, mesh=mesh, in_specs=in_specs, out_specs=out_specs, check_vma=False)
```

profile of v0, /device:TPU:0, one launch (start us, length us, event | category | flops | bytes accessed | tf_op | source)
XLA Modules:
  0.0 342.1 jit_solution(14312674388534561637)
XLA Ops:
  7.2 1.0 convert_reduce_fusion.1
  8.2 0.9 convolution_reduce_fusion
  9.1 1.9 fusion.30
  11.1 0.5 collective-permute-start
  11.6 5.0 %collective-permute-start.1 = (bf16[1,128,1,256]{1,3,2,0:T(8,128)(2,1)S(1)}, bf16[1,128,1,256]{1,3,2,0:T(8,128)(2,1)S(1)}, u32[]{:S(2)}, u32[]{:S(2)}) collective-permute-start(bf16[1,128,1,256]{1,3,2,0:T(8,128)(2,1)S(1)} %get-tuple-element.42), channel_id=1, source_target_pairs={{2,0},{4,2},{6,4},{8,6},{10,8},{12,10},{14,12},{16,14},{18,16},{20... | collective-permute-start | bytes 196616 | tf_op jit(solution)/shard_map/ppermute | solution.py:22
  16.9 1.2 fusion.177
  18.2 4.4 %collective-permute-start.5 = (bf16[1,128,2,256]{1,3,2,0:T(8,128)(2,1)S(1)}, bf16[1,128,2,256]{1,3,2,0:T(8,128)(2,1)S(1)}, u32[]{:S(2)}, u32[]{:S(2)}) collective-permute-start(bf16[1,128,2,256]{1,3,2,0:T(8,128)(2,1)S(1)} %get-tuple-element.44), channel_id=1, source_target_pairs={{2,0},{4,2},{6,4},{8,6},{10,8},{12,10},{14,12},{16,14},{18,16},{20... | collective-permute-start | bytes 393224 | tf_op jit(solution)/shard_map/ppermute | solution.py:22
  22.6 4.7 %all_gather.7 = bf16[2,128,128]{2,1,0:T(8,128)(2,1)} all-gather(bf16[1,128,128]{2,1,0:T(8,128)(2,1)S(1)} %copy-done.10), channel_id=1, replica_groups=mesh['az'=16,'el'=2] {'el'}, dimensions={0}, use_global_device_ids=true | all-gather | bytes 98304 | tf_op jit(solution)/shard_map/all_gather | solution.py:121
  27.4 0.3 copy.223
  28.1 0.5 copy-done.22
  28.6 1.1 convolution_select_fusion.3
  29.9 1.0 reshape.182
  31.5 0.8 copy-done.19
  32.4 1.1 convolution_select_fusion.1
  33.7 1.0 reshape.186
  34.6 3.1 fusion.170
  38.0 0.9 convolution_bitcast_fusion.6
  40.2 0.4 copy-done.2
  40.5 0.3 convolution_bitcast_fusion.15
  41.6 4.4 %collective-permute-start.7 = (bf16[1,128,1,256]{1,3,2,0:T(8,128)(2,1)S(1)}, bf16[1,128,1,256]{1,3,2,0:T(8,128)(2,1)S(1)}, u32[]{:S(2)}, u32[]{:S(2)}) collective-permute-start(bf16[1,128,1,256]{1,3,2,0:T(8,128)(2,1)S(1)} %get-tuple-element.38), channel_id=1, source_target_pairs={{2,0},{4,2},{6,4},{8,6},{10,8},{12,10},{14,12},{16,14},{18,16},{20... | collective-permute-start | bytes 196616 | tf_op jit(solution)/shard_map/ppermute | solution.py:22
  46.0 4.4 %collective-permute-start.3 = (bf16[1,128,2,256]{1,3,2,0:T(8,128)(2,1)S(1)}, bf16[1,128,2,256]{1,3,2,0:T(8,128)(2,1)S(1)}, u32[]{:S(2)}, u32[]{:S(2)}) collective-permute-start(bf16[1,128,2,256]{1,3,2,0:T(8,128)(2,1)S(1)} %get-tuple-element.40), channel_id=1, source_target_pairs={{2,0},{4,2},{6,4},{8,6},{10,8},{12,10},{14,12},{16,14},{18,16},{20... | collective-permute-start | bytes 393224 | tf_op jit(solution)/shard_map/ppermute | solution.py:22
  51.1 0.9 pad_maximum_fusion.1
  52.1 0.3 copy.224
  52.6 1.1 convolution_select_fusion
  53.9 1.0 reshape.188
  54.8 2.0 convert_reduce_fusion
  57.2 37.2 %all-reduce.2 = (f32[24,128]{1,0:T(8,128)S(1)}, f32[4,128]{1,0:T(4,128)S(1)}) all-reduce(f32[24,128]{1,0:T(8,128)S(1)} %convolution_bitcast_fusion.21, f32[4,128]{1,0:T(4,128)S(1)} %fusion.135), channel_id=1, replica_groups=mesh['az'=16,'el'=2] {'az','el'}, use_global_device_ids=true, to_apply=%region_5.6 | all-reduce | flops 3584 | bytes 28672 | tf_op jit(solution)/shard_map/psum | solution.py:172
  94.5 0.6 broadcast_multiply_fusion.2
  95.2 0.5 copy-done.11
  96.4 0.9 convolution_bitcast_fusion.7
  97.3 0.9 convolution_bitcast_fusion.8
  98.3 0.9 convolution_bitcast_fusion.2
  99.2 0.9 convolution_bitcast_fusion.4
  100.7 0.8 copy-done.20
  101.5 1.1 convolution_select_fusion.2
  102.8 1.0 reshape.184
  103.8 1.2 fusion.15
  105.1 0.9 convolution_bitcast_fusion.20
  107.0 0.9 pad_maximum_fusion.2
  107.9 0.6 broadcast_multiply_fusion.3
  108.6 11.7 %all-gather = bf16[2,128,6,256]{3,1,2,0:T(8,128)(2,1)S(1)} all-gather(bf16[1,128,6,256]{3,1,2,0:T(8,128)(2,1)S(1)} %copy.130), channel_id=2, replica_groups=mesh['az'=16,'el'=2] {'el'}, dimensions={0}, use_global_device_ids=true | all-gather | bytes 1179648 | tf_op jit(solution)/shard_map/all_gather | solution.py:120
  120.3 0.7 fusion.10
  121.0 0.7 copy.180
  121.8 70.7 %all-reduce.7.cloned.1.call-done = f32[128,128]{1,0:T(8,128)} async-done(((f32[128,128]{1,0:T(8,128)}), f32[128,128]{1,0:T(8,128)}) %all-reduce.7.cloned.1.call-update) | async-done | bytes 65552 | tf_op jit(solution)/shard_map/psum | solution.py:138
  192.5 1.5 multiply_bitcast_fusion
  193.9 138.5 %all-reduce.9.cloned.1.call-done = (f32[3,3,128,128]{3,2,1,0:T(8,128)}, f32[3,3,128,128]{3,2,1,0:T(8,128)}) async-done(((f32[3,3,128,128]{3,2,1,0:T(8,128)}, f32[3,3,128,128]{3,2,1,0:T(8,128)}), (f32[3,3,128,128]{3,2,1,0:T(8,128)}, f32[3,3,128,128]{3,2,1,0:T(8,128)})) %all-reduce.9.cloned.1.call-update) | async-done | bytes 1179664 | tf_op jit(solution)/shard_map/psum | solution.py:172
  332.4 2.0 broadcast_multiply_fusion
  334.4 0.9 broadcast_multiply_fusion.1
  (103 shorter events, 7.9 us)
Async XLA Ops:
  7.2 20.9 %copy-start = (bf16[3,3,128,128]{3,2,1,0:T(8,128)(2,1)S(1)}, bf16[3,3,128,128]{3,2,1,0:T(8,128)(2,1)}, u32[]{:S(2)}) copy-start(bf16[3,3,128,128]{3,2,1,0:T(8,128)(2,1)} %param.13) | copy-start | bytes 884740
  7.2 185.3 %all-reduce.7.cloned.1.call-start = ((), (), s32[]{:S(2)}) async-start(), calls=%async_computation | async-start | bytes 131072 | tf_op jit(solution)/shard_map/psum | solution.py:138
  9.1 7.5 %copy-start.17 = (bf16[1,12,6,256]{3,2,1,0:T(8,128)(2,1)S(1)}, bf16[1,12,6,256]{3,2,1,0:T(8,128)(2,1)}, u32[]{:S(2)}) copy-start(bf16[1,12,6,256]{3,2,1,0:T(8,128)(2,1)} %param.17) | copy-start | bytes 110596
  9.1 7.5 %copy-start.18 = (bf16[12,128]{1,0:T(8,128)(2,1)S(1)}, bf16[12,128]{1,0:T(8,128)(2,1)}, u32[]{:S(2)}) copy-start(bf16[12,128]{1,0:T(8,128)(2,1)} %param.16) | copy-start | bytes 9220
  9.1 7.8 %copy-start.10 = (bf16[1,128,128]{2,1,0:T(8,128)(2,1)S(1)}, bf16[1,128,128]{2,1,0:T(8,128)(2,1)}, u32[]{:S(2)}) copy-start(bf16[1,128,128]{2,1,0:T(8,128)(2,1)} %param.15) | copy-start | bytes 98308
  11.1 16.2 %copy-start.1 = (bf16[128,6,256]{0,2,1:T(8,128)(2,1)}, bf16[128,6,256]{0,2,1:T(8,128)(2,1)S(1)}, u32[]{:S(2)}) copy-start(bf16[128,6,256]{0,2,1:T(8,128)(2,1)S(1)} %get-tuple-element.47) | copy-start | bytes 1179652
  11.1 16.2 %collective-permute-start = (bf16[1,128,1,256]{1,3,2,0:T(8,128)(2,1)S(1)}, bf16[1,128,1,256]{1,3,2,0:T(8,128)(2,1)S(1)}, u32[]{:S(2)}, u32[]{:S(2)}) collective-permute-start(bf16[1,128,1,256]{1,3,2,0:T(8,128)(2,1)S(1)} %get-tuple-element.41), channel_id=1, source_target_pairs={{0,2},{2,4},{4,6},{6,8},{8,10},{10,12},{12,14},{14,16},{16,18},{18... | collective-permute-start | bytes 196616 | tf_op jit(solution)/shard_map/ppermute | solution.py:19
  11.6 15.7 %collective-permute-start.1 = (bf16[1,128,1,256]{1,3,2,0:T(8,128)(2,1)S(1)}, bf16[1,128,1,256]{1,3,2,0:T(8,128)(2,1)S(1)}, u32[]{:S(2)}, u32[]{:S(2)}) collective-permute-start(bf16[1,128,1,256]{1,3,2,0:T(8,128)(2,1)S(1)} %get-tuple-element.42), channel_id=1, source_target_pairs={{2,0},{4,2},{6,4},{8,6},{10,8},{12,10},{14,12},{16,14},{18,16},{20... | collective-permute-start | bytes 196616 | tf_op jit(solution)/shard_map/ppermute | solution.py:22
  18.1 12.8 %collective-permute-start.4 = (bf16[1,128,2,256]{1,3,2,0:T(8,128)(2,1)S(1)}, bf16[1,128,2,256]{1,3,2,0:T(8,128)(2,1)S(1)}, u32[]{:S(2)}, u32[]{:S(2)}) collective-permute-start(bf16[1,128,2,256]{1,3,2,0:T(8,128)(2,1)S(1)} %get-tuple-element.43), channel_id=1, source_target_pairs={{0,2},{2,4},{4,6},{6,8},{8,10},{10,12},{12,14},{14,16},{16,18},{18... | collective-permute-start | bytes 393224 | tf_op jit(solution)/shard_map/ppermute | solution.py:19
  18.2 12.7 %collective-permute-start.5 = (bf16[1,128,2,256]{1,3,2,0:T(8,128)(2,1)S(1)}, bf16[1,128,2,256]{1,3,2,0:T(8,128)(2,1)S(1)}, u32[]{:S(2)}, u32[]{:S(2)}) collective-permute-start(bf16[1,128,2,256]{1,3,2,0:T(8,128)(2,1)S(1)} %get-tuple-element.44), channel_id=1, source_target_pairs={{2,0},{4,2},{6,4},{8,6},{10,8},{12,10},{14,12},{16,14},{18,16},{20... | collective-permute-start | bytes 393224 | tf_op jit(solution)/shard_map/ppermute | solution.py:22
  27.3 0.6 copy-start.15
  27.9 0.7 copy-start.22
  31.4 1.0 copy-start.19
  39.5 1.0 copy-start.2
  40.9 9.6 %copy-start.16 = (bf16[1,128,1,256]{1,3,2,0:T(8,128)(2,1)S(1)}, bf16[1,128,1,256]{1,3,2,0:T(8,128)(2,1)}, u32[]{:S(2)}) copy-start(bf16[1,128,1,256]{1,3,2,0:T(8,128)(2,1)} %copy-done.15) | copy-start | bytes 196612
  41.5 10.5 %collective-permute-start.6 = (bf16[1,128,1,256]{1,3,2,0:T(8,128)(2,1)S(1)}, bf16[1,128,1,256]{1,3,2,0:T(8,128)(2,1)S(1)}, u32[]{:S(2)}, u32[]{:S(2)}) collective-permute-start(bf16[1,128,1,256]{1,3,2,0:T(8,128)(2,1)S(1)} %get-tuple-element.37), channel_id=1, source_target_pairs={{0,2},{2,4},{4,6},{6,8},{8,10},{10,12},{12,14},{14,16},{16,18},{18... | collective-permute-start | bytes 196616 | tf_op jit(solution)/shard_map/ppermute | solution.py:19
  41.6 10.4 %collective-permute-start.7 = (bf16[1,128,1,256]{1,3,2,0:T(8,128)(2,1)S(1)}, bf16[1,128,1,256]{1,3,2,0:T(8,128)(2,1)S(1)}, u32[]{:S(2)}, u32[]{:S(2)}) collective-permute-start(bf16[1,128,1,256]{1,3,2,0:T(8,128)(2,1)S(1)} %get-tuple-element.38), channel_id=1, source_target_pairs={{2,0},{4,2},{6,4},{8,6},{10,8},{12,10},{14,12},{16,14},{18,16},{20... | collective-permute-start | bytes 196616 | tf_op jit(solution)/shard_map/ppermute | solution.py:22
  46.0 49.1 %collective-permute-start.2 = (bf16[1,128,2,256]{1,3,2,0:T(8,128)(2,1)S(1)}, bf16[1,128,2,256]{1,3,2,0:T(8,128)(2,1)S(1)}, u32[]{:S(2)}, u32[]{:S(2)}) collective-permute-start(bf16[1,128,2,256]{1,3,2,0:T(8,128)(2,1)S(1)} %get-tuple-element.39), channel_id=1, source_target_pairs={{0,2},{2,4},{4,6},{6,8},{8,10},{10,12},{12,14},{14,16},{16,18},{18... | collective-permute-start | bytes 393224 | tf_op jit(solution)/shard_map/ppermute | solution.py:19
  46.0 49.1 %collective-permute-start.3 = (bf16[1,128,2,256]{1,3,2,0:T(8,128)(2,1)S(1)}, bf16[1,128,2,256]{1,3,2,0:T(8,128)(2,1)S(1)}, u32[]{:S(2)}, u32[]{:S(2)}) collective-permute-start(bf16[1,128,2,256]{1,3,2,0:T(8,128)(2,1)S(1)} %get-tuple-element.40), channel_id=1, source_target_pairs={{2,0},{4,2},{6,4},{8,6},{10,8},{12,10},{14,12},{16,14},{18,16},{20... | collective-permute-start | bytes 393224 | tf_op jit(solution)/shard_map/ppermute | solution.py:22
  54.8 2.2 copy-start.21
  95.1 0.7 copy-start.11
  95.1 0.7 copy-start.13
  100.6 1.0 copy-start.20
  103.8 2.3 copy-start.14
  105.1 1.4 copy-start.6
  105.1 1.4 copy-start.7
  105.1 1.4 copy-start.12
  106.0 0.8 copy-start.4
  106.1 0.9 copy-start.5
  106.1 0.9 copy-start.8
  106.1 226.3 %all-reduce.9.cloned.1.call-start = ((), (), s32[]{:S(2)}) async-start(), calls=%async_computation.1 | async-start | bytes 2359296 | tf_op jit(solution)/shard_map/psum | solution.py:172
  108.5 11.9 %copy-start.9 = (bf16[2,128,128]{2,1,0:T(8,128)(2,1)S(1)}, bf16[2,128,128]{2,1,0:T(8,128)(2,1)}, u32[]{:S(2)}) copy-start(bf16[2,128,128]{2,1,0:T(8,128)(2,1)} %all_gather.7) | copy-start | bytes 196612
  332.4 2.0 copy-start.3
Sparse Core Ops, SparseCore 0:
  106.2 86.2 all-reduce.6
  199.5 132.8 all-reduce.8
where the time goes:
time: 343 us; the launch traced here: 342 us
  waiting for transfers between devices  209 us (61%)
  blocking collectives  53.6 us (16%)
  matrix products  19.5 us (6%)
  starting transfers between devices  19 us (6%)
  other arithmetic  15.1 us (4%)
  between operations  14.6 us (4%)
  local copies, waits for them, and re-layouts  11 us (3%)
    psum x1, waiting for transfers between devices, shards(): lax.psum((second_kernel_partial, first_kernel_partial, input_local, embed...  138 us
    psum x1, waiting for transfers between devices, shards(): join_total = lax.psum(join_local, 'az')  70.7 us
    psum x1, blocking collectives, shards(): lax.psum((second_kernel_partial, first_kernel_partial, input_local, embed...  37.2 us
    ppermute x4, starting transfers between devices, padded_2(): lax.ppermute(lax.slice_in_dim(block, 0, width, axis=dim), axis, backward)  18.3 us
    all_gather x1, blocking collectives, shards(): lax.all_gather(final_state[None], 'el', axis=0, tiled=True)  11.7 us
    dot_general x18, matrix products, kernel_gradient_of(): jnp.einsum('niar,noar->io', window, upstream, preferred_element_type=jnp....  8.68 us
  transfers between devices with their start and end apart: 10, of which 2 were waited for; matrix products, arithmetic and copies ran while one was open for 5% of the time, Pallas kernels for 0%

commit v1 on v0

--- a/solution.py
+++ b/solution.py
@@ -135,7 +135,7 @@
     join_local = jnp.einsum(
         "biar,boar->io", final_state, joined_back, preferred_element_type=jnp.float32
     )
-    join_total = lax.psum(join_local, "az")
+    join_total = jnp.sum(lax.all_gather(join_local, "az"), axis=0)
     grad_two = jnp.einsum(
         "io,boar->biar", group_weight, joined_back, preferred_element_type=jnp.float32
     )

time: 343 us -> 209 us (0.61)
  waiting for transfers between devices: 209 us -> 74.6 us
    psum x1 -> x0, waiting for transfers between devices: 70.7 us -> none  [shards(): join_total = lax.psum(join_local, 'az')]
    psum x1, waiting for transfers between devices: 138 us -> 74.6 us  [shards(): lax.psum((second_kernel_partial, first_kernel_partial, input_local, embed...]
  transfers between devices with their start and end apart: 10 -> 10, of which waited for: 2 -> 1; matrix products, arithmetic and copies ran while one was open for 5% -> 9% of each run, Pallas kernels for 0% -> 0%
where the time goes in v1:
time: 209 us; the launch traced here: 208 us
  waiting for transfers between devices  74.6 us (36%)
  blocking collectives  54.4 us (26%)
  matrix products  20.1 us (10%)
  starting transfers between devices  19 us (9%)
  between operations  16.1 us (8%)
  other arithmetic  13.9 us (7%)
  local copies, waits for them, and re-layouts  10.2 us (5%)
    psum x1, waiting for transfers between devices, shards(): lax.psum((second_kernel_partial, first_kernel_partial, input_local, embed...  74.6 us
    psum x1, blocking collectives, shards(): lax.psum((second_kernel_partial, first_kernel_partial, input_local, embed...  37.4 us
    ppermute x4, starting transfers between devices, padded_2(): lax.ppermute(lax.slice_in_dim(block, 0, width, axis=dim), axis, backward)  18.3 us
    all_gather x1, blocking collectives, shards(): lax.all_gather(final_state[None], 'el', axis=0, tiled=True)  12.3 us
    dot_general x18, matrix products, kernel_gradient_of(): jnp.einsum('niar,noar->io', window, upstream, preferred_element_type=jnp....  9.3 us
    unnamed x55, local copies, waits for them, and re-layouts  5.09 us
    all_gather x1, blocking collectives, shards(): lax.all_gather(join_weight, 'el', axis=0, tiled=True)  4.68 us
    conv_general_dilated x4, matrix products, convolve_partial(): lax.conv_general_dilated(padded, kernel, (1, 1), 'VALID', rhs_dilation=(d...  4.5 us
  transfers between devices with their start and end apart: 10, of which 1 were waited for; matrix products, arithmetic and copies ran while one was open for 9% of the time, Pallas kernels for 0%

profile of v1, /device:TPU:0, one launch (start us, length us, event | category | flops | bytes accessed | tf_op | source)
XLA Modules:
  0.0 208.3 jit_solution(16677643427880231782)
XLA Ops:
  8.1 1.0 convert_reduce_fusion.1
  9.0 0.9 convolution_reduce_fusion
  10.0 1.9 fusion.30
  11.9 0.5 collective-permute-start
  12.4 5.0 %collective-permute-start.1 = (bf16[1,128,1,256]{1,3,2,0:T(8,128)(2,1)S(1)}, bf16[1,128,1,256]{1,3,2,0:T(8,128)(2,1)S(1)}, u32[]{:S(2)}, u32[]{:S(2)}) collective-permute-start(bf16[1,128,1,256]{1,3,2,0:T(8,128)(2,1)S(1)} %get-tuple-element.42), channel_id=1, source_target_pairs={{2,0},{4,2},{6,4},{8,6},{10,8},{12,10},{14,12},{16,14},{18,16},{20... | collective-permute-start | bytes 196616 | tf_op jit(solution)/shard_map/ppermute | solution.py:22
  17.8 1.2 fusion.177
  19.0 4.4 %collective-permute-start.5 = (bf16[1,128,2,256]{1,3,2,0:T(8,128)(2,1)S(1)}, bf16[1,128,2,256]{1,3,2,0:T(8,128)(2,1)S(1)}, u32[]{:S(2)}, u32[]{:S(2)}) collective-permute-start(bf16[1,128,2,256]{1,3,2,0:T(8,128)(2,1)S(1)} %get-tuple-element.44), channel_id=1, source_target_pairs={{2,0},{4,2},{6,4},{8,6},{10,8},{12,10},{14,12},{16,14},{18,16},{20... | collective-permute-start | bytes 393224 | tf_op jit(solution)/shard_map/ppermute | solution.py:22
  23.4 4.7 %all_gather.13 = bf16[2,128,128]{2,1,0:T(8,128)(2,1)} all-gather(bf16[1,128,128]{2,1,0:T(8,128)(2,1)S(1)} %copy-done.13), channel_id=1, replica_groups=mesh['az'=16,'el'=2] {'el'}, dimensions={0}, use_global_device_ids=true | all-gather | bytes 98304 | tf_op jit(solution)/shard_map/all_gather | solution.py:121
  28.2 0.3 copy.223
  28.9 0.5 copy-done.25
  29.5 1.1 convolution_select_fusion.3
  30.8 1.0 reshape.191
  32.4 0.8 copy-done.22
  33.2 1.1 convolution_select_fusion.1
  34.5 1.0 reshape.195
  35.5 3.1 %fusion.170 = (bf16[1,128,6,256]{1,3,2,0:T(8,128)(2,1)S(1)}, f32[1,128,6,256]{1,3,2,0:T(8,128)}, bf16[1,128,6,256]{1,3,2,0:T(8,128)(2,1)S(1)}) fusion(f32[1,128,6,256]{1,3,2,0:T(8,128)} %get-tuple-element.46, f32[6,1,264,128]{3,2,0,1:T(8,128)} %reshape.195, f32[6,1,264,128]{3,2,0,1:T(8,128)} %reshape.191, f32[6,256,128]{2,1,0:T(8,128)} %get-tuple-element.48), kind=kLoop, calls=%fused_computation.226 | loop fusion | flops 2555904 | bytes 4718592 | tf_op jit(solution)/shard_map/convert_element_type | solution.py:153
  38.8 0.9 convolution_bitcast_fusion.6
  40.0 0.3 convolution_bitcast_fusion.16
  40.7 0.3 convolution_bitcast_fusion.19
  41.0 0.4 copy-done.4
  41.3 0.3 convolution_bitcast_fusion.15
  42.4 4.4 %collective-permute-start.7 = (bf16[1,128,1,256]{1,3,2,0:T(8,128)(2,1)S(1)}, bf16[1,128,1,256]{1,3,2,0:T(8,128)(2,1)S(1)}, u32[]{:S(2)}, u32[]{:S(2)}) collective-permute-start(bf16[1,128,1,256]{1,3,2,0:T(8,128)(2,1)S(1)} %get-tuple-element.38), channel_id=1, source_target_pairs={{2,0},{4,2},{6,4},{8,6},{10,8},{12,10},{14,12},{16,14},{18,16},{20... | collective-permute-start | bytes 196616 | tf_op jit(solution)/shard_map/ppermute | solution.py:22
  46.8 4.4 %collective-permute-start.3 = (bf16[1,128,2,256]{1,3,2,0:T(8,128)(2,1)S(1)}, bf16[1,128,2,256]{1,3,2,0:T(8,128)(2,1)S(1)}, u32[]{:S(2)}, u32[]{:S(2)}) collective-permute-start(bf16[1,128,2,256]{1,3,2,0:T(8,128)(2,1)S(1)} %get-tuple-element.40), channel_id=1, source_target_pairs={{2,0},{4,2},{6,4},{8,6},{10,8},{12,10},{14,12},{16,14},{18,16},{20... | collective-permute-start | bytes 393224 | tf_op jit(solution)/shard_map/ppermute | solution.py:22
  51.9 0.9 pad_maximum_fusion.1
  52.9 0.3 copy.224
  53.4 1.1 convolution_select_fusion
  54.7 1.0 reshape.197
  56.3 0.9 convolution_bitcast_fusion.5
  57.3 0.9 convolution_bitcast_fusion.7
  58.2 0.9 convolution_bitcast_fusion.8
  59.1 0.9 convolution_bitcast_fusion.2
  60.1 0.9 convolution_bitcast_fusion.4
  61.6 0.7 copy-done.17
  63.3 0.9 pad_maximum_fusion.2
  64.3 1.1 convolution_select_fusion.2
  65.8 0.9 convolution_bitcast_fusion.20
  67.1 1.5 convert_reduce_fusion
  69.1 37.4 %all-reduce.2 = (f32[24,128]{1,0:T(8,128)S(1)}, f32[4,128]{1,0:T(4,128)S(1)}) all-reduce(f32[24,128]{1,0:T(8,128)S(1)} %convolution_bitcast_fusion.21, f32[4,128]{1,0:T(4,128)S(1)} %fusion.135), channel_id=1, replica_groups=mesh['az'=16,'el'=2] {'az','el'}, use_global_device_ids=true, to_apply=%region_5.6 | all-reduce | flops 3584 | bytes 28672 | tf_op jit(solution)/shard_map/psum | solution.py:172
  106.4 0.6 broadcast_multiply_fusion.3
  107.0 0.6 broadcast_multiply_fusion.2
  107.8 12.3 %all-gather = bf16[2,128,6,256]{3,1,2,0:T(8,128)(2,1)S(1)} all-gather(bf16[1,128,6,256]{3,1,2,0:T(8,128)(2,1)S(1)} %copy.130), channel_id=2, replica_groups=mesh['az'=16,'el'=2] {'el'}, dimensions={0}, use_global_device_ids=true | all-gather | bytes 1179648 | tf_op jit(solution)/shard_map/all_gather | solution.py:120
  120.1 0.7 fusion.10
  120.8 0.7 copy.180
  121.5 74.6 %all-reduce.6.cloned.1.call-done = (f32[3,3,128,128]{3,2,1,0:T(8,128)}, f32[3,3,128,128]{3,2,1,0:T(8,128)}) async-done(((f32[3,3,128,128]{3,2,1,0:T(8,128)}, f32[3,3,128,128]{3,2,1,0:T(8,128)}), (f32[3,3,128,128]{3,2,1,0:T(8,128)}, f32[3,3,128,128]{3,2,1,0:T(8,128)})) %all-reduce.6.cloned.1.call-update) | async-done | bytes 1179664 | tf_op jit(solution)/shard_map/psum | solution.py:172
  196.1 2.0 broadcast_multiply_fusion
  198.1 0.9 broadcast_multiply_fusion.1
  199.0 1.3 reduce_sum.42
  200.3 0.6 multiply_bitcast_fusion
  (110 shorter events, 7.9 us)
Async XLA Ops:
  8.0 20.9 %copy-start = (bf16[3,3,128,128]{3,2,1,0:T(8,128)(2,1)S(1)}, bf16[3,3,128,128]{3,2,1,0:T(8,128)(2,1)}, u32[]{:S(2)}) copy-start(bf16[3,3,128,128]{3,2,1,0:T(8,128)(2,1)} %param.13) | copy-start | bytes 884740
  8.0 188.1 %all-reduce.6.cloned.1.call-start = ((), (), s32[]{:S(2)}) async-start(), calls=%async_computation.1 | async-start | bytes 2359296 | tf_op jit(solution)/shard_map/psum | solution.py:172
  9.9 7.5 %copy-start.20 = (bf16[1,12,6,256]{3,2,1,0:T(8,128)(2,1)S(1)}, bf16[1,12,6,256]{3,2,1,0:T(8,128)(2,1)}, u32[]{:S(2)}) copy-start(bf16[1,12,6,256]{3,2,1,0:T(8,128)(2,1)} %param.17) | copy-start | bytes 110596
  9.9 7.5 %copy-start.21 = (bf16[12,128]{1,0:T(8,128)(2,1)S(1)}, bf16[12,128]{1,0:T(8,128)(2,1)}, u32[]{:S(2)}) copy-start(bf16[12,128]{1,0:T(8,128)(2,1)} %param.16) | copy-start | bytes 9220
  9.9 7.8 %copy-start.13 = (bf16[1,128,128]{2,1,0:T(8,128)(2,1)S(1)}, bf16[1,128,128]{2,1,0:T(8,128)(2,1)}, u32[]{:S(2)}) copy-start(bf16[1,128,128]{2,1,0:T(8,128)(2,1)} %param.15) | copy-start | bytes 98308
  11.9 16.2 %copy-start.3 = (bf16[128,6,256]{0,2,1:T(8,128)(2,1)}, bf16[128,6,256]{0,2,1:T(8,128)(2,1)S(1)}, u32[]{:S(2)}) copy-start(bf16[128,6,256]{0,2,1:T(8,128)(2,1)S(1)} %get-tuple-element.47) | copy-start | bytes 1179652
  11.9 16.2 %collective-permute-start = (bf16[1,128,1,256]{1,3,2,0:T(8,128)(2,1)S(1)}, bf16[1,128,1,256]{1,3,2,0:T(8,128)(2,1)S(1)}, u32[]{:S(2)}, u32[]{:S(2)}) collective-permute-start(bf16[1,128,1,256]{1,3,2,0:T(8,128)(2,1)S(1)} %get-tuple-element.41), channel_id=1, source_target_pairs={{0,2},{2,4},{4,6},{6,8},{8,10},{10,12},{12,14},{14,16},{16,18},{18... | collective-permute-start | bytes 196616 | tf_op jit(solution)/shard_map/ppermute | solution.py:19
  12.4 15.7 %collective-permute-start.1 = (bf16[1,128,1,256]{1,3,2,0:T(8,128)(2,1)S(1)}, bf16[1,128,1,256]{1,3,2,0:T(8,128)(2,1)S(1)}, u32[]{:S(2)}, u32[]{:S(2)}) collective-permute-start(bf16[1,128,1,256]{1,3,2,0:T(8,128)(2,1)S(1)} %get-tuple-element.42), channel_id=1, source_target_pairs={{2,0},{4,2},{6,4},{8,6},{10,8},{12,10},{14,12},{16,14},{18,16},{20... | collective-permute-start | bytes 196616 | tf_op jit(solution)/shard_map/ppermute | solution.py:22
  18.9 12.8 %collective-permute-start.4 = (bf16[1,128,2,256]{1,3,2,0:T(8,128)(2,1)S(1)}, bf16[1,128,2,256]{1,3,2,0:T(8,128)(2,1)S(1)}, u32[]{:S(2)}, u32[]{:S(2)}) collective-permute-start(bf16[1,128,2,256]{1,3,2,0:T(8,128)(2,1)S(1)} %get-tuple-element.43), channel_id=1, source_target_pairs={{0,2},{2,4},{4,6},{6,8},{8,10},{10,12},{12,14},{14,16},{16,18},{18... | collective-permute-start | bytes 393224 | tf_op jit(solution)/shard_map/ppermute | solution.py:19
  19.0 12.7 %collective-permute-start.5 = (bf16[1,128,2,256]{1,3,2,0:T(8,128)(2,1)S(1)}, bf16[1,128,2,256]{1,3,2,0:T(8,128)(2,1)S(1)}, u32[]{:S(2)}, u32[]{:S(2)}) collective-permute-start(bf16[1,128,2,256]{1,3,2,0:T(8,128)(2,1)S(1)} %get-tuple-element.44), channel_id=1, source_target_pairs={{2,0},{4,2},{6,4},{8,6},{10,8},{12,10},{14,12},{16,14},{18,16},{20... | collective-permute-start | bytes 393224 | tf_op jit(solution)/shard_map/ppermute | solution.py:22
  28.1 0.6 copy-start.18
  28.8 0.7 copy-start.25
  32.2 1.0 copy-start.22
  40.3 1.0 copy-start.4
  41.7 9.6 %copy-start.19 = (bf16[1,128,1,256]{1,3,2,0:T(8,128)(2,1)S(1)}, bf16[1,128,1,256]{1,3,2,0:T(8,128)(2,1)}, u32[]{:S(2)}) copy-start(bf16[1,128,1,256]{1,3,2,0:T(8,128)(2,1)} %copy-done.18) | copy-start | bytes 196612
  42.3 10.5 %collective-permute-start.6 = (bf16[1,128,1,256]{1,3,2,0:T(8,128)(2,1)S(1)}, bf16[1,128,1,256]{1,3,2,0:T(8,128)(2,1)S(1)}, u32[]{:S(2)}, u32[]{:S(2)}) collective-permute-start(bf16[1,128,1,256]{1,3,2,0:T(8,128)(2,1)S(1)} %get-tuple-element.37), channel_id=1, source_target_pairs={{0,2},{2,4},{4,6},{6,8},{8,10},{10,12},{12,14},{14,16},{16,18},{18... | collective-permute-start | bytes 196616 | tf_op jit(solution)/shard_map/ppermute | solution.py:19
  42.4 10.4 %collective-permute-start.7 = (bf16[1,128,1,256]{1,3,2,0:T(8,128)(2,1)S(1)}, bf16[1,128,1,256]{1,3,2,0:T(8,128)(2,1)S(1)}, u32[]{:S(2)}, u32[]{:S(2)}) collective-permute-start(bf16[1,128,1,256]{1,3,2,0:T(8,128)(2,1)S(1)} %get-tuple-element.38), channel_id=1, source_target_pairs={{2,0},{4,2},{6,4},{8,6},{10,8},{12,10},{14,12},{16,14},{18,16},{20... | collective-permute-start | bytes 196616 | tf_op jit(solution)/shard_map/ppermute | solution.py:22
  46.8 8.8 %collective-permute-start.2 = (bf16[1,128,2,256]{1,3,2,0:T(8,128)(2,1)S(1)}, bf16[1,128,2,256]{1,3,2,0:T(8,128)(2,1)S(1)}, u32[]{:S(2)}, u32[]{:S(2)}) collective-permute-start(bf16[1,128,2,256]{1,3,2,0:T(8,128)(2,1)S(1)} %get-tuple-element.39), channel_id=1, source_target_pairs={{0,2},{2,4},{4,6},{6,8},{8,10},{10,12},{12,14},{14,16},{16,18},{18... | collective-permute-start | bytes 393224 | tf_op jit(solution)/shard_map/ppermute | solution.py:19
  46.8 8.8 %collective-permute-start.3 = (bf16[1,128,2,256]{1,3,2,0:T(8,128)(2,1)S(1)}, bf16[1,128,2,256]{1,3,2,0:T(8,128)(2,1)S(1)}, u32[]{:S(2)}, u32[]{:S(2)}) collective-permute-start(bf16[1,128,2,256]{1,3,2,0:T(8,128)(2,1)S(1)} %get-tuple-element.40), channel_id=1, source_target_pairs={{2,0},{4,2},{6,4},{8,6},{10,8},{12,10},{14,12},{16,14},{18,16},{20... | collective-permute-start | bytes 393224 | tf_op jit(solution)/shard_map/ppermute | solution.py:22
  55.6 0.6 copy-start.14
  55.6 0.7 copy-start.16
  61.4 0.9 copy-start.17
  61.4 1.2 copy-start.9
  61.4 1.2 copy-start.10
  61.5 1.1 copy-start.15
  62.3 0.9 copy-start.6
  62.3 0.9 copy-start.7
  62.3 0.9 copy-start.8
  62.3 0.9 copy-start.11
  63.3 1.0 copy-start.23
  64.2 134.8 %all-gather.4.cloned.1.call-start = ((), (), s32[]{:S(2)}) async-start(), calls=%async_computation | async-start | bytes 1114112 | tf_op jit(solution)/shard_map/all_gather | solution.py:138
  65.7 1.1 copy-start.1
  65.8 1.3 copy-start.2
  67.1 1.7 copy-start.24
  68.8 51.3 %copy-start.12 = (bf16[2,128,128]{2,1,0:T(8,128)(2,1)S(1)}, bf16[2,128,128]{2,1,0:T(8,128)(2,1)}, u32[]{:S(2)}) copy-start(bf16[2,128,128]{2,1,0:T(8,128)(2,1)} %all_gather.13) | copy-start | bytes 196612
  196.1 2.0 copy-start.5
Sparse Core Ops, SparseCore 0:
  64.3 131.7 all-reduce.5
Sparse Core Ops, SparseCore 1:
  67.4 38.3 all-gather.3
